TPU v7x, 32 devices: a whole 2x2x4 slice. The times are simulated.
32 devices in a mesh: dp: 8 (over z, y), expert: 4 (over x, core).
Axes of the slice: x: 2, y: 2, z: 4, core: 2. Of those that a mesh axis runs over, the one named last changes fastest.
Arguments:
- hidden_in: float32 [4, 2560, 1536], P('expert', 'dp'), may hold values from -6 to 6
- gain_attn: float32 [1536], replicated, may hold values from 0.5 to 1.5
- w_query: bfloat16 [1536, 1536], replicated, may hold values from -0.15625 to 0.15625
- w_key: bfloat16 [1536, 512], replicated, may hold values from -0.15625 to 0.15625
- w_value: bfloat16 [1536, 512], replicated, may hold values from -0.15625 to 0.15625
- w_output: bfloat16 [1536, 1536], replicated, may hold values from -1.25 to 1.25
- gain_mlp: float32 [1536], replicated, may hold values from 0.5 to 1.5
- w_router: bfloat16 [1536, 40], replicated, may hold values from -0.078125 to 0.078125
- w_gate: bfloat16 [40, 1536, 512], P('expert'), may hold values from -0.15625 to 0.15625
- w_up: bfloat16 [40, 1536, 512], P('expert'), may hold values from -0.15625 to 0.15625
- w_down: bfloat16 [40, 512, 1536], P('expert'), may hold values from -1 to 1
- expert_ids: int32 [4, 2560, 8], P('expert', 'dp'), may hold values from 0 to 39, all different within a row
- slot_order: int32 [4, 8, 2560], P('expert', 'dp'), may hold values from 0 to 2559, each once within a row
- grad_out: float32 [4, 2560, 1536], P('expert', 'dp'), may hold values from -6 to 6
Outputs:
- hidden_out: float32 [4, 2560, 1536], P('expert', 'dp')
- grad_in: float32 [4, 2560, 1536], P('expert', 'dp')
- grad_gain_attn: float32 [1536], P(('dp', 'expert'))
- grad_query: float32 [1536, 1536], P(('dp', 'expert'))
- grad_key: float32 [1536, 512], P(('dp', 'expert'))
- grad_value: float32 [1536, 512], P(('dp', 'expert'))
- grad_output: float32 [1536, 1536], P(('dp', 'expert'))
- grad_gain_mlp: float32 [1536], P(('dp', 'expert'))
- grad_router: float32 [1536, 40], P(('dp', 'expert'))
- grad_gate: float32 [40, 1536, 512], P('expert', 'dp')
- grad_up: float32 [40, 1536, 512], P('expert', 'dp')
- grad_down: float32 [40, 512, 1536], P('expert', 'dp')
Inputs may be any that keep to these rules, and one draw needn't show every extreme that they name: `expert_ids`: each token names 8 different experts. `slot_order`: for every sequence and block, the 2560 ranks of the block's pairs are each of 0 to 2559 once.
All inputs are finite; a program needn't handle non-finite values.
Results may differ from a plain program's by a relative error of at most 0.019.
Values may be sent and summed in bfloat16 or wider, within the bound.
A program may use at most 320 MiB of HBM per device.

v0:
```python
import math
import jax
import jax.numpy as jnp
from jax import lax
from jax.sharding import PartitionSpec as P

HEADS = 24
KV_HEADS = 8
HEAD_DIM = 64
EPS = 1e-05
MASKED = -1e30


def rotary_tables(positions):
    half = HEAD_DIM // 2
    frequency = jnp.exp(-math.log(10000.0) * jnp.arange(half, dtype=jnp.float32) * 2.0 / HEAD_DIM)
    angles = positions.astype(jnp.float32)[:, None] * frequency[None, :]
    return (jnp.cos(angles)[:, None, :], jnp.sin(angles)[:, None, :])


def rotate(values, cosine, sine):
    half = values.shape[-1] // 2
    first = values[..., :half]
    second = values[..., half:]
    return jnp.concatenate(
        [first * cosine - second * sine, second * cosine + first * sine], axis=-1
    )


def rotate_back(values, cosine, sine):
    half = values.shape[-1] // 2
    first = values[..., :half]
    second = values[..., half:]
    return jnp.concatenate(
        [first * cosine + second * sine, second * cosine - first * sine], axis=-1
    )


def assign_slots(row_chosen, row_ranks, all_experts, capacity):
    pairs = row_chosen.shape[0]
    by_rank = jnp.zeros((pairs,), jnp.int32).at[row_ranks].set(jnp.arange(pairs, dtype=jnp.int32))
    ordered = row_chosen[by_rank]
    table = (ordered[:, None] == jnp.arange(all_experts, dtype=jnp.int32)[None, :]).astype(
        jnp.int32
    )
    before = jnp.sum(table * (jnp.cumsum(table, axis=0) - 1), axis=1)
    slot = before[row_ranks]
    target = jnp.where(slot < capacity, row_chosen * capacity + slot, all_experts * capacity)
    owner = (
        jnp.full((all_experts * capacity,), pairs, jnp.int32)
        .at[target]
        .set(jnp.arange(pairs, dtype=jnp.int32), mode="drop")
    )
    return (target, owner)


def body(
    hidden_in,
    gain_attn,
    w_query,
    w_key,
    w_value,
    w_output,
    gain_mlp,
    w_router,
    w_gate,
    w_up,
    w_down,
    expert_ids,
    slot_order,
    grad_out,
):
    inputs = hidden_in[0]
    cotangent = grad_out[0]
    chosen = expert_ids[0]
    tokens, width = inputs.shape
    top = chosen.shape[1]
    local_experts = w_gate.shape[0]
    peers = lax.axis_size("expert")
    all_experts = local_experts * peers
    pairs = tokens * top
    capacity = pairs // all_experts
    shards = lax.axis_size("dp")
    index = lax.axis_index("dp")
    length = shards * tokens
    block = math.gcd(length, 512)
    groups = HEADS // KV_HEADS
    scale = HEAD_DIM ** (-0.5)
    query_pos = index * tokens + jnp.arange(tokens, dtype=jnp.int32)
    cosine, sine = rotary_tables(query_pos)
    count = ((index + 1) * tokens + block - 1) // block
    inv_one = lax.rsqrt(jnp.mean(inputs * inputs, axis=-1, keepdims=True) + EPS)
    normed = (inputs * inv_one * gain_attn).astype(jnp.bfloat16)
    query_pre = jnp.dot(normed, w_query, preferred_element_type=jnp.float32).reshape(
        tokens, HEADS, HEAD_DIM
    )
    queries = rotate(query_pre, cosine, sine).astype(jnp.bfloat16)
    key_pre = jnp.dot(normed, w_key, preferred_element_type=jnp.float32).reshape(
        tokens, KV_HEADS, HEAD_DIM
    )
    keys_low = rotate(key_pre, cosine, sine).astype(jnp.bfloat16)
    values_low = (
        jnp.dot(normed, w_value, preferred_element_type=jnp.float32)
        .astype(jnp.bfloat16)
        .reshape(tokens, KV_HEADS, HEAD_DIM)
    )
    keys_all, values_all = (
        lax.all_gather(keys_low, "dp", axis=0, tiled=True),
        lax.all_gather(values_low, "dp", axis=0, tiled=True),
    )
    query_groups = queries.reshape(tokens, KV_HEADS, groups, HEAD_DIM)

    def block_scores(key_block, start):
        raw = (
            jnp.einsum(
                "qkgd,skd->kgqs", query_groups, key_block, preferred_element_type=jnp.float32
            )
            * scale
        )
        key_pos = start + jnp.arange(block, dtype=jnp.int32)
        allowed = key_pos[None, :] <= query_pos[:, None]
        return jnp.where(allowed, raw, MASKED)

    def stats_step(step, carry):
        running, total = carry
        scores = block_scores(
            lax.dynamic_slice_in_dim(keys_all, step * block, block, 0), step * block
        )
        newest = jnp.maximum(running, jnp.max(scores, axis=-1))
        total = total * jnp.exp(running - newest) + jnp.sum(
            jnp.exp(scores - newest[..., None]), axis=-1
        )
        return (newest, total)

    stat_init = (
        jnp.full((KV_HEADS, groups, tokens), MASKED, jnp.float32),
        jnp.zeros((KV_HEADS, groups, tokens), jnp.float32),
    )
    running, total = lax.fori_loop(0, count, stats_step, stat_init)
    log_total = running + jnp.log(total)

    def output_step(step, accum):
        start = step * block
        scores = block_scores(lax.dynamic_slice_in_dim(keys_all, start, block, 0), start)
        probs = jnp.exp(scores - log_total[..., None]).astype(jnp.bfloat16)
        value_block = lax.dynamic_slice_in_dim(values_all, start, block, 0)
        return accum + jnp.einsum(
            "kgqs,skd->qkgd", probs, value_block, preferred_element_type=jnp.float32
        )

    attended_groups = lax.fori_loop(
        0, count, output_step, jnp.zeros((tokens, KV_HEADS, groups, HEAD_DIM), jnp.float32)
    )
    attended = attended_groups.reshape(tokens, HEADS * HEAD_DIM)
    attended_low = attended.astype(jnp.bfloat16)
    branch = jnp.dot(attended_low, w_output, preferred_element_type=jnp.float32)
    middle = inputs + branch
    inv_two = lax.rsqrt(jnp.mean(middle * middle, axis=-1, keepdims=True) + EPS)
    normed_two = (middle * inv_two * gain_mlp).astype(jnp.bfloat16)
    logits = jnp.dot(normed_two, w_router, preferred_element_type=jnp.float32)
    onehot = (chosen[:, :, None] == jnp.arange(all_experts, dtype=jnp.int32)[None, None, :]).astype(
        jnp.float32
    )
    picked = jnp.sum(onehot * logits[:, None, :], axis=-1)
    gates = jax.nn.softmax(picked, axis=-1)
    target, owner = assign_slots(chosen.reshape(pairs), slot_order[0, 0], all_experts, capacity)
    valid = owner < pairs
    source = jnp.minimum(owner, pairs - 1)
    rows_send = jnp.where(valid[:, None], normed_two[source // top], 0).reshape(
        peers, local_experts, capacity, width
    )
    received = lax.all_to_all(rows_send, "expert", split_axis=0, concat_axis=0, tiled=True)
    gate_pre = jnp.einsum("necd,edf->necf", received, w_gate, preferred_element_type=jnp.float32)
    up_pre = jnp.einsum("necd,edf->necf", received, w_up, preferred_element_type=jnp.float32)
    hidden = (jax.nn.silu(gate_pre) * up_pre).astype(jnp.bfloat16)
    result = jnp.einsum(
        "necf,efd->necd", hidden, w_down, preferred_element_type=jnp.float32
    ).astype(jnp.bfloat16)
    returned = lax.all_to_all(result, "expert", split_axis=0, concat_axis=0, tiled=True)
    returned, received, gate_pre, up_pre = (returned, received, gate_pre, up_pre)
    zero_row = jnp.zeros((1, width), jnp.bfloat16)
    pair_out = jnp.concatenate([returned.reshape(all_experts * capacity, width), zero_row], axis=0)[
        target
    ].reshape(tokens, top, width)
    mixed = jnp.einsum("tk,tkd->td", gates, pair_out, preferred_element_type=jnp.float32)
    hidden_out = middle + mixed
    dy_pairs = (
        (gates[:, :, None] * cotangent[:, None, :]).astype(jnp.bfloat16).reshape(pairs, width)
    )
    dy_send = jnp.where(valid[:, None], dy_pairs[source], 0).reshape(
        peers, local_experts, capacity, width
    )
    dy_received = lax.all_to_all(dy_send, "expert", split_axis=0, concat_axis=0, tiled=True)
    sigmoid_gate = jax.nn.sigmoid(gate_pre)
    silu_gate = gate_pre * sigmoid_gate
    hidden = (silu_gate * up_pre).astype(jnp.bfloat16)
    grad_down_part = jnp.einsum(
        "necf,necd->efd", hidden, dy_received, preferred_element_type=jnp.float32
    )
    d_hidden = jnp.einsum("necd,efd->necf", dy_received, w_down, preferred_element_type=jnp.float32)
    d_gate = (d_hidden * up_pre * sigmoid_gate * (1.0 + gate_pre * (1.0 - sigmoid_gate))).astype(
        jnp.bfloat16
    )
    d_up = (d_hidden * silu_gate).astype(jnp.bfloat16)
    grad_gate_part = jnp.einsum(
        "necd,necf->edf", received, d_gate, preferred_element_type=jnp.float32
    )
    grad_up_part = jnp.einsum("necd,necf->edf", received, d_up, preferred_element_type=jnp.float32)
    gate_total, up_total, down_total = (
        lax.psum_scatter(
            grad_gate_part.astype(jnp.bfloat16), "dp", scatter_dimension=1, tiled=True
        ).astype(jnp.float32),
        lax.psum_scatter(
            grad_up_part.astype(jnp.bfloat16), "dp", scatter_dimension=1, tiled=True
        ).astype(jnp.float32),
        lax.psum_scatter(
            grad_down_part.astype(jnp.bfloat16), "dp", scatter_dimension=1, tiled=True
        ).astype(jnp.float32),
    )
    d_rows = jnp.einsum("necf,edf->necd", d_gate, w_gate, preferred_element_type=jnp.float32)
    d_rows = (
        d_rows + jnp.einsum("necf,edf->necd", d_up, w_up, preferred_element_type=jnp.float32)
    ).astype(jnp.bfloat16)
    d_back = lax.all_to_all(d_rows, "expert", split_axis=0, concat_axis=0, tiled=True)
    d_pairs = jnp.concatenate([d_back.reshape(all_experts * capacity, width), zero_row], axis=0)[
        target
    ].reshape(tokens, top, width)
    d_normed_two = jnp.sum(d_pairs, axis=1, dtype=jnp.float32)
    d_gates = jnp.einsum("td,tkd->tk", cotangent, pair_out, preferred_element_type=jnp.float32)
    d_picked = gates * (d_gates - jnp.sum(gates * d_gates, axis=-1, keepdims=True))
    d_logits = jnp.sum(onehot * d_picked[:, :, None], axis=1).astype(jnp.bfloat16)
    grad_router_part = jnp.einsum(
        "td,te->de", normed_two, d_logits, preferred_element_type=jnp.float32
    )
    d_normed_two = d_normed_two + jnp.einsum(
        "te,de->td", d_logits, w_router, preferred_element_type=jnp.float32
    )
    scaled_two = d_normed_two * gain_mlp
    grad_gain_mlp_part = jnp.sum(d_normed_two * middle * inv_two, axis=0)
    d_middle = (
        cotangent
        + inv_two * scaled_two
        - middle * inv_two**3 * jnp.mean(middle * scaled_two, axis=-1, keepdims=True)
    )
    d_branch = d_middle.astype(jnp.bfloat16)
    grad_output_part = jnp.einsum(
        "tf,td->fd", attended_low, d_branch, preferred_element_type=jnp.float32
    )
    d_attended = jnp.einsum(
        "td,fd->tf", d_branch, w_output, preferred_element_type=jnp.float32
    ).astype(jnp.bfloat16)
    d_groups = d_attended.reshape(tokens, KV_HEADS, groups, HEAD_DIM)
    delta = jnp.einsum(
        "qkgd,qkgd->kgq", d_groups, attended_groups, preferred_element_type=jnp.float32
    )
    keys_back, values_back = (
        lax.all_gather(keys_low, "dp", axis=0, tiled=True),
        lax.all_gather(values_low, "dp", axis=0, tiled=True),
    )

    def grad_step(step, carry):
        d_query, d_keys, d_values = carry
        start = step * block
        key_block = lax.dynamic_slice_in_dim(keys_back, start, block, 0)
        value_block = lax.dynamic_slice_in_dim(values_back, start, block, 0)
        scores = block_scores(key_block, start)
        probs = jnp.exp(scores - log_total[..., None])
        probs_low = probs.astype(jnp.bfloat16)
        d_probs = jnp.einsum(
            "qkgd,skd->kgqs", d_groups, value_block, preferred_element_type=jnp.float32
        )
        d_scores = (probs * (d_probs - delta[..., None])).astype(jnp.bfloat16)
        d_query = d_query + jnp.einsum(
            "kgqs,skd->qkgd", d_scores, key_block, preferred_element_type=jnp.float32
        )
        key_part = jnp.einsum(
            "kgqs,qkgd->skd", d_scores, query_groups, preferred_element_type=jnp.float32
        )
        value_part = jnp.einsum(
            "kgqs,qkgd->skd", probs_low, d_groups, preferred_element_type=jnp.float32
        )
        d_keys = lax.dynamic_update_slice_in_dim(
            d_keys, lax.dynamic_slice_in_dim(d_keys, start, block, 0) + key_part, start, 0
        )
        d_values = lax.dynamic_update_slice_in_dim(
            d_values, lax.dynamic_slice_in_dim(d_values, start, block, 0) + value_part, start, 0
        )
        return (d_query, d_keys, d_values)

    grad_init = (
        jnp.zeros((tokens, KV_HEADS, groups, HEAD_DIM), jnp.float32),
        jnp.zeros((length, KV_HEADS, HEAD_DIM), jnp.float32),
        jnp.zeros((length, KV_HEADS, HEAD_DIM), jnp.float32),
    )
    d_query, d_keys, d_values = lax.fori_loop(0, count, grad_step, grad_init)
    key_sum, value_sum = (
        lax.psum_scatter(
            (d_keys * scale).reshape(length, KV_HEADS * HEAD_DIM).astype(jnp.bfloat16),
            "dp",
            scatter_dimension=0,
            tiled=True,
        ).astype(jnp.float32),
        lax.psum_scatter(
            d_values.reshape(length, KV_HEADS * HEAD_DIM).astype(jnp.bfloat16),
            "dp",
            scatter_dimension=0,
            tiled=True,
        ).astype(jnp.float32),
    )
    d_query_low = (
        rotate_back((d_query * scale).reshape(tokens, HEADS, HEAD_DIM), cosine, sine)
        .astype(jnp.bfloat16)
        .reshape(tokens, HEADS * HEAD_DIM)
    )
    d_key_low = (
        rotate_back(key_sum.reshape(tokens, KV_HEADS, HEAD_DIM), cosine, sine)
        .astype(jnp.bfloat16)
        .reshape(tokens, KV_HEADS * HEAD_DIM)
    )
    d_value_low = value_sum.astype(jnp.bfloat16)
    grad_query_part = jnp.einsum(
        "td,tf->df", normed, d_query_low, preferred_element_type=jnp.float32
    )
    grad_key_part = jnp.einsum("td,tf->df", normed, d_key_low, preferred_element_type=jnp.float32)
    grad_value_part = jnp.einsum(
        "td,tf->df", normed, d_value_low, preferred_element_type=jnp.float32
    )
    d_normed = jnp.einsum("tf,df->td", d_query_low, w_query, preferred_element_type=jnp.float32)
    d_normed = d_normed + jnp.einsum(
        "tf,df->td", d_key_low, w_key, preferred_element_type=jnp.float32
    )
    d_normed = d_normed + jnp.einsum(
        "tf,df->td", d_value_low, w_value, preferred_element_type=jnp.float32
    )
    scaled_one = d_normed * gain_attn
    grad_gain_attn_part = jnp.sum(d_normed * inputs * inv_one, axis=0)
    grad_in = (
        d_middle
        + inv_one * scaled_one
        - inputs * inv_one**3 * jnp.mean(inputs * scaled_one, axis=-1, keepdims=True)
    )
    dense = (
        lax.psum_scatter(grad_gain_attn_part, ("dp", "expert"), scatter_dimension=0, tiled=True),
        lax.psum_scatter(grad_query_part, ("dp", "expert"), scatter_dimension=0, tiled=True),
        lax.psum_scatter(grad_key_part, ("dp", "expert"), scatter_dimension=0, tiled=True),
        lax.psum_scatter(grad_value_part, ("dp", "expert"), scatter_dimension=0, tiled=True),
        lax.psum_scatter(grad_output_part, ("dp", "expert"), scatter_dimension=0, tiled=True),
        lax.psum_scatter(grad_gain_mlp_part, ("dp", "expert"), scatter_dimension=0, tiled=True),
        lax.psum_scatter(grad_router_part, ("dp", "expert"), scatter_dimension=0, tiled=True),
    )
    return (
        hidden_out[None],
        grad_in[None],
        dense[0],
        dense[1],
        dense[2],
        dense[3],
        dense[4],
        dense[5],
        dense[6],
        gate_total,
        up_total,
        down_total,
    )


def solution(mesh):
    in_specs = (
        P("expert", "dp", None),
        P(),
        P(),
        P(),
        P(),
        P(),
        P(),
        P(),
        P("expert", None, None),
        P("expert", None, None),
        P("expert", None, None),
        P("expert", "dp", None),
        P("expert", "dp", None),
        P("expert", "dp", None),
    )
    out_specs = (
        P("expert", "dp", None),
        P("expert", "dp", None),
        P(("dp", "expert")),
        P(("dp", "expert"), None),
        P(("dp", "expert"), None),
        P(("dp", "expert"), None),
        P(("dp", "expert"), None),
        P(("dp", "expert")),
        P(("dp", "expert"), None),
        P("expert", "dp", None),
        P("expert", "dp", None),
        P("expert", "dp", None),
    )
    return jax.shard_map(body, mesh=mesh, in_specs=in_specs, out_specs=out_specs, check_vma=False)
```

profile of v0, /device:TPU:0, one launch (start us, length us, event | category | flops | bytes accessed | tf_op | source)
XLA Modules:
  0.0 2534.0 jit_solution(5355342469741384523)
XLA Ops:
  24.0 9.9 scatter_custom_fusion
  34.3 13.6 gather_fusion
  48.0 11.5 reduce-window.6
  60.5 13.6 gather_fusion.1
  74.8 9.9 scatter_custom_fusion.1
  99.2 9.0 all-gather.5.cloned.1.call-done
  115.0 9.9 while.39
  124.9 70.6 %all-gather.3.cloned.1.call-done = bf16[2560,8,64]{2,1,0:T(8,128)(2,1)} async-done(((bf16[320,8,64]{2,1,0:T(8,128)(2,1)}), bf16[2560,8,64]{2,1,0:T(8,128)(2,1)}) %all-gather.3.cloned.1.call-update) | async-done | bytes 2621456 | tf_op jit(solution)/shard_map/all_gather | solution.py:109
  204.0 9.5 while.40
  204.2 9.3 bitcast_add_fusion.5
  222.0 9.6 gather_fusion.2
  231.6 6.9 broadcast_select_fusion.1
  238.5 95.0 %all_to_all.20 = bf16[4,10,64,1536]{3,2,1,0:T(8,128)(2,1)} all-to-all(bf16[4,10,64,1536]{3,2,1,0:T(8,128)(2,1)} %broadcast_select_fusion.1), channel_id=1, replica_groups=mesh['dp'=8,'expert'=4] {'expert'}, dimensions={0} | all-to-all | bytes 15728640 | tf_op jit(solution)/shard_map/all_to_all | solution.py:172
  333.6 14.2 fusion.62
  347.8 16.7 fusion.86
  364.5 13.7 convert_bitcast_fusion
  378.3 7.2 copy.90
  393.1 85.8 %all-to-all-done.1 = bf16[4,10,64,1536]{3,2,1,0:T(8,128)(2,1)} async-done(((bf16[4,10,64,1536]{3,2,1,0:T(8,128)(2,1)}), bf16[4,10,64,1536]{3,2,1,0:T(8,128)(2,1)}, u32[]{:S(2)}, u32[]{:S(2)}) %all-to-all-start.1) | async-done | bytes 7864352 | tf_op jit(solution)/shard_map/all_to_all | solution.py:179
  485.8 20.9 gather_fusion.3
  506.6 8.0 fusion.70
  526.1 20.6 gather_fusion.4
  546.7 7.0 broadcast_select_fusion
  553.7 95.3 %all_to_all.21 = bf16[4,10,64,1536]{3,2,1,0:T(8,128)(2,1)} all-to-all(bf16[4,10,64,1536]{3,2,1,0:T(8,128)(2,1)} %broadcast_select_fusion), channel_id=1, replica_groups=mesh['dp'=8,'expert'=4] {'expert'}, dimensions={0} | all-to-all | bytes 15728640 | tf_op jit(solution)/shard_map/all_to_all | solution.py:193
  649.0 15.8 fusion.84
  664.8 11.8 fusion.56
  676.7 15.9 fusion.69
  692.6 7.3 copy.93
  712.7 80.4 %all-to-all-done.3 = bf16[4,10,64,1536]{3,2,1,0:T(8,128)(2,1)} async-done(((bf16[4,10,64,1536]{3,2,1,0:T(8,128)(2,1)}), bf16[4,10,64,1536]{3,2,1,0:T(8,128)(2,1)}, u32[]{:S(2)}, u32[]{:S(2)}) %all-to-all-start.3) | async-done | bytes 7864352 | tf_op jit(solution)/shard_map/all_to_all | solution.py:224
  793.1 6.8 concatenate.30
  800.0 20.8 gather_fusion.5
  820.8 8.7 convert_reduce_fusion
  850.3 26.7 %while.41 = (s32[]{:T(128)}, f32[320,8,3,64]{0,3,2,1:T(8,128)}, f32[2560,8,64]{0,2,1:T(8,128)}, f32[2560,8,64]{0,2,1:T(8,128)}, s32[]{:T(128)}, /*index=5*/bf16[...) while((s32[]{:T(128)}, f32[320,8,3,64]{0,3,2,1:T(8,128)}, ...), condition=%wide.region_21.22_spmd.clone, body=%wide.region_20.21_spmd.clone.sunk | while | flops 2557084416 | bytes 89326328 | solution.py:295
  860.0 6.9 fusion.214
  897.3 10.8 bitcast_convert_fusion
  908.2 10.7 bitcast_convert_fusion.2
  919.0 10.7 bitcast_convert_fusion.1
  929.8 167.0 %reduce-scatter.31.cloned.1.call-done = bf16[320,512]{1,0:T(8,128)(2,1)} async-done(((bf16[2560,512]{1,0:T(8,128)(2,1)}), bf16[320,512]{1,0:T(8,128)(2,1)}) %reduce-scatter.31.cloned.1.call-update) | async-done | bytes 327696
  1101.8 67.6 %reduce-scatter.33.cloned.1.call-done = bf16[320,512]{1,0:T(8,128)(2,1)} async-done(((bf16[2560,512]{1,0:T(8,128)(2,1)}), bf16[320,512]{1,0:T(8,128)(2,1)}) %reduce-scatter.33.cloned.1.call-update) | async-done | bytes 327696
  1173.5 8.1 fusion.113
  1190.4 78.4 %reduce-scatter.35.cloned.1.call-done = f32[48,40]{1,0:T(8,128)} async-done(((f32[1536,40]{1,0:T(8,128)}), f32[48,40]{1,0:T(8,128)}) %reduce-scatter.35.cloned.1.call-update) | async-done | bytes 7696
  1279.0 46.3 %all-reduce.4 = (f32[1536]{0:T(1024)}, f32[1536]{0:T(1024)}) all-reduce(f32[1536]{0:T(1024)} %get-tuple-element.315, f32[1536]{0:T(1024)} %get-tuple-element.313), channel_id=4, replica_groups=mesh['dp'=8,'expert'=4] {'dp','expert'}, use_global_device_ids=true, to_apply=%region_26.27.clone | all-reduce | flops 3072 | bytes 24576
  1332.4 191.1 %reduce-scatter.29.cloned.1.call-done = bf16[10,64,1536]{2,1,0:T(8,128)(2,1)} async-done(((bf16[10,512,1536]{2,1,0:T(8,128)(2,1)}), bf16[10,64,1536]{2,1,0:T(8,128)(2,1)}) %reduce-scatter.29.cloned.1.call-update) | async-done | bytes 1966096 | tf_op jit(solution)/shard_map/reduce_scatter | solution.py:216
  1527.5 249.8 %reduce-scatter.25.cloned.1.call-done = bf16[10,192,512]{2,1,0:T(8,128)(2,1)} async-done(((bf16[10,1536,512]{2,1,0:T(8,128)(2,1)}), bf16[10,192,512]{2,1,0:T(8,128)(2,1)}) %reduce-scatter.25.cloned.1.call-update) | async-done | bytes 1966096 | tf_op jit(solution)/shard_map/reduce_scatter | solution.py:210
  1781.3 249.8 %reduce-scatter.27.cloned.1.call-done = bf16[10,192,512]{2,1,0:T(8,128)(2,1)} async-done(((bf16[10,1536,512]{2,1,0:T(8,128)(2,1)}), bf16[10,192,512]{2,1,0:T(8,128)(2,1)}) %reduce-scatter.27.cloned.1.call-update) | async-done | bytes 1966096 | tf_op jit(solution)/shard_map/reduce_scatter | solution.py:213
  2035.1 102.6 %reduce-scatter.19.cloned.1.call-done = f32[48,512]{1,0:T(8,128)} async-done(((f32[1536,512]{1,0:T(8,128)}), f32[48,512]{1,0:T(8,128)}) %reduce-scatter.19.cloned.1.call-update) | async-done | bytes 98320 | tf_op jit(solution)/shard_map/reduce_scatter | solution.py:345
  2137.8 106.3 %reduce-scatter.21.cloned.1.call-done = f32[48,512]{1,0:T(8,128)} async-done(((f32[1536,512]{1,0:T(8,128)}), f32[48,512]{1,0:T(8,128)}) %reduce-scatter.21.cloned.1.call-update) | async-done | bytes 98320 | tf_op jit(solution)/shard_map/reduce_scatter | solution.py:346
  2244.1 140.9 %reduce-scatter.23.cloned.1.call-done = f32[48,1536]{1,0:T(8,128)} async-done(((f32[1536,1536]{1,0:T(8,128)}), f32[48,1536]{1,0:T(8,128)}) %reduce-scatter.23.cloned.1.call-update) | async-done | bytes 294928 | tf_op jit(solution)/shard_map/reduce_scatter | solution.py:347
  2385.0 141.9 %reduce-scatter.17.cloned.1.call-done = f32[48,1536]{1,0:T(8,128)} async-done(((f32[1536,1536]{1,0:T(8,128)}), f32[48,1536]{1,0:T(8,128)}) %reduce-scatter.17.cloned.1.call-update) | async-done | bytes 294928 | tf_op jit(solution)/shard_map/reduce_scatter | solution.py:344
  (273 shorter events, 212.4 us)
Async XLA Ops:
  7.2 12.0 copy-start
  7.2 7.3 copy-start.5
  7.2 7.3 copy-start.41
  7.2 101.0 %all-gather.5.cloned.1.call-start = ((), (), s32[]{:S(2)}) async-start(), calls=%async_computation.15 | async-start | bytes 5898240 | tf_op jit(solution)/shard_map/all_gather | solution.py:108
  10.9 8.2 copy-start.49
  19.1 176.5 %all-gather.3.cloned.1.call-start = ((), (), s32[]{:S(2)}) async-start(), calls=%async_computation.14 | async-start | bytes 5898240 | tf_op jit(solution)/shard_map/all_gather | solution.py:109
  84.8 146.8 %copy-start.45 = (pred[4,10,64]{2,1,0:T(8,128)(4,1)}, pred[4,10,64]{2,1,0:T(8,128)(4,1)S(1)}, u32[]{:S(2)}) copy-start(pred[4,10,64]{2,1,0:T(8,128)(4,1)S(1)} %broadcast_in_dim.67) | copy-start | bytes 7684
  84.8 6.8 copy-start.13
  213.5 6.9 copy-start.3
  213.5 6.9 copy-start.53
  216.2 5.5 copy-start.47
  221.1 10.5 copy-start.55
  222.0 170.0 %copy-start.1 = (bf16[320,1536]{1,0:T(8,128)(2,1)}, bf16[320,1536]{1,0:T(8,128)(2,1)S(1)}, u32[]{:S(2)}) copy-start(bf16[320,1536]{1,0:T(8,128)(2,1)S(1)} %multiply_convert_fusion.1) | copy-start | bytes 2949124
  385.4 6.0 copy-start.52
  385.4 6.6 copy-start.33
  385.4 7.0 copy-start.38
  385.4 93.5 %all-to-all-start.1 = ((bf16[4,10,64,1536]{3,2,1,0:T(8,128)(2,1)}), bf16[4,10,64,1536]{3,2,1,0:T(8,128)(2,1)}, u32[]{:S(2)}, u32[]{:S(2)}) async-start(bf16[4,10,64,1536]{3,2,1,0:T(8,128)(2,1)} %copy.90), calls=%async_computation.1 | async-start | bytes 15728640 | tf_op jit(solution)/shard_map/all_to_all | solution.py:179
  485.8 20.9 copy-start.16
  526.1 20.6 copy-start.46
  699.9 5.7 copy-start.40
  699.9 6.6 copy-start.44
  699.9 6.6 copy-start.60
  699.9 6.6 copy-start.39
  699.9 93.2 %all-to-all-start.3 = ((bf16[4,10,64,1536]{3,2,1,0:T(8,128)(2,1)}), bf16[4,10,64,1536]{3,2,1,0:T(8,128)(2,1)}, u32[]{:S(2)}, u32[]{:S(2)}) async-start(bf16[4,10,64,1536]{3,2,1,0:T(8,128)(2,1)} %copy.93), calls=%async_computation.3 | async-start | bytes 15728640 | tf_op jit(solution)/shard_map/all_to_all | solution.py:224
  705.6 391.2 %reduce-scatter.31.cloned.1.call-start = ((), (), s32[]{:S(2)}) async-start(), calls=%async_computation.23 | async-start | bytes 2949120
  793.1 6.8 copy-start.43
  820.8 8.7 copy-start.9
  820.8 8.7 copy-start.34
  820.8 8.7 copy-start.35
  820.8 8.7 copy-start.48
  820.8 8.7 copy-start.56
  829.5 6.1 slice-start
  885.9 283.5 %reduce-scatter.33.cloned.1.call-start = ((), (), s32[]{:S(2)}) async-start(), calls=%async_computation.24 | async-start | bytes 2949120
  894.7 374.1 %reduce-scatter.35.cloned.1.call-start = ((), (), s32[]{:S(2)}) async-start(), calls=%async_computation.25 | async-start | bytes 811008
  897.3 626.3 %reduce-scatter.29.cloned.1.call-start = ((), (), s32[]{:S(2)}) async-start(), calls=%async_computation.22 | async-start | bytes 17694720 | tf_op jit(solution)/shard_map/reduce_scatter | solution.py:216
  908.2 869.1 %reduce-scatter.25.cloned.1.call-start = ((), (), s32[]{:S(2)}) async-start(), calls=%async_computation.20 | async-start | bytes 17694720 | tf_op jit(solution)/shard_map/reduce_scatter | solution.py:210
  918.9 1112.2 %reduce-scatter.27.cloned.1.call-start = ((), (), s32[]{:S(2)}) async-start(), calls=%async_computation.21 | async-start | bytes 17694720 | tf_op jit(solution)/shard_map/reduce_scatter | solution.py:213
  929.7 168.4 %copy-start.27 = (f32[320,32]{0,1:T(8,128)S(1)}, f32[320,32]{0,1:T(8,128)}, u32[]{:S(2)}) copy-start(f32[320,32]{0,1:T(8,128)} %copy-done.25) | copy-start | bytes 122884
  929.7 168.4 %copy-start.31 = (f32[320,32]{0,1:T(8,128)S(1)}, f32[320,32]{0,1:T(8,128)}, u32[]{:S(2)}) copy-start(f32[320,32]{0,1:T(8,128)} %copy-done.29) | copy-start | bytes 122884
  929.7 169.3 %copy-start.14 = (bf16[1,320,1536]{2,1,0:T(8,128)(2,1)S(1)}, bf16[1,320,1536]{2,1,0:T(8,128)(2,1)}, u32[]{:S(2)}) copy-start(bf16[1,320,1536]{2,1,0:T(8,128)(2,1)} %copy-done.12) | copy-start | bytes 2949124
  929.7 1208.1 %reduce-scatter.19.cloned.1.call-start = ((), (), s32[]{:S(2)}) async-start(), calls=%async_computation.17 | async-start | bytes 3244032 | tf_op jit(solution)/shard_map/reduce_scatter | solution.py:345
  1101.7 67.7 %copy-start.7 = (f32[1,320,1536]{2,1,0:T(8,128)S(1)}, f32[1,320,1536]{2,1,0:T(8,128)}, u32[]{:S(2)}) copy-start(f32[1,320,1536]{2,1,0:T(8,128)} %param.20) | copy-start | bytes 5898244
  1101.7 67.7 %copy-start.42 = (f32[1536]{0:T(1024)S(1)}, f32[1536]{0:T(1024)}, u32[]{:S(2)}) copy-start(f32[1536]{0:T(1024)} %param.21) | copy-start | bytes 18436
  1101.7 67.7 %copy-start.50 = (f32[320]{0:T(512)S(1)}, f32[320]{0:T(512)}, u32[]{:S(2)}) copy-start(f32[320]{0:T(512)} %copy-done.49) | copy-start | bytes 3844
  1101.7 1142.4 %reduce-scatter.21.cloned.1.call-start = ((), (), s32[]{:S(2)}) async-start(), calls=%async_computation.18 | async-start | bytes 3244032 | tf_op jit(solution)/shard_map/reduce_scatter | solution.py:346
  1173.3 1211.8 %reduce-scatter.23.cloned.1.call-start = ((), (), s32[]{:S(2)}) async-start(), calls=%async_computation.19 | async-start | bytes 9732096 | tf_op jit(solution)/shard_map/reduce_scatter | solution.py:347
  1181.6 1345.4 %reduce-scatter.17.cloned.1.call-start = ((), (), s32[]{:S(2)}) async-start(), calls=%async_computation.16 | async-start | bytes 9732096 | tf_op jit(solution)/shard_map/reduce_scatter | solution.py:344
  1276.2 52.2 %copy-start.58 = (f32[320]{0:T(512)S(1)}, f32[320]{0:T(512)}, u32[]{:S(2)}) copy-start(f32[320]{0:T(512)} %get-tuple-element.395) | copy-start | bytes 3844
  (30 other events, 79.5 us)
Sparse Core Ops, SparseCore 0:
  19.2 88.9 all-gather.4
  110.9 84.5 all-gather.2
  886.0 210.6 reduce-scatter.30
  1100.2 69.2 reduce-scatter.32
  1174.4 94.3 reduce-scatter.34
  1272.2 251.2 reduce-scatter.28
  1527.1 250.1 reduce-scatter.24
  1780.9 250.2 reduce-scatter.26
  2037.1 100.5 reduce-scatter.18
  2143.6 100.4 reduce-scatter.20
  2250.6 134.4 reduce-scatter.22
  2392.4 134.5 reduce-scatter.16
where the time goes:
time: 2540 us; the launch traced here: 2530 us
  waiting for transfers between devices  1740 us (69%)
  blocking collectives  237 us (9%)
  matrix products  220 us (9%)
  local copies, waits for them, and re-layouts  212 us (8%)
  other arithmetic  95.4 us (4%)
    unnamed x15, waiting for transfers between devices  313 us
    reduce_scatter x1, waiting for transfers between devices, body(): lax.psum_scatter(grad_up_part.astype(jnp.bfloat16), 'dp', scatter_dimensi...  250 us
    reduce_scatter x1, waiting for transfers between devices, body(): lax.psum_scatter(grad_gate_part.astype(jnp.bfloat16), 'dp', scatter_dimen...  250 us
    reduce_scatter x1, waiting for transfers between devices, body(): lax.psum_scatter(grad_down_part.astype(jnp.bfloat16), 'dp', scatter_dimen...  191 us
    reduce_scatter x1, waiting for transfers between devices, body(): lax.psum_scatter(grad_query_part, ('dp', 'expert'), scatter_dimension=0,...  142 us
    reduce_scatter x1, waiting for transfers between devices, body(): lax.psum_scatter(grad_output_part, ('dp', 'expert'), scatter_dimension=0,...  141 us
    reduce_scatter x1, waiting for transfers between devices, body(): lax.psum_scatter(grad_value_part, ('dp', 'expert'), scatter_dimension=0,...  106 us
    reduce_scatter x1, waiting for transfers between devices, body(): lax.psum_scatter(grad_key_part, ('dp', 'expert'), scatter_dimension=0, ti...  103 us
  transfers between devices with their start and end apart: 14, of which 14 were waited for; matrix products, arithmetic and copies ran while one was open for 8% of the time, Pallas kernels for 0%

commit v1 on v0

--- a/solution.py
+++ b/solution.py
@@ -106,7 +106,9 @@
     )
     keys_all, values_all = (
         lax.all_gather(keys_low, "dp", axis=0, tiled=True),
-        lax.all_gather(values_low, "dp", axis=0, tiled=True),
+        jnp.concatenate(
+            lax.all_to_all(jnp.stack([values_low] * lax.axis_size("dp")), "dp", 0, 0), axis=0
+        ),
     )
     query_groups = queries.reshape(tokens, KV_HEADS, groups, HEAD_DIM)
 

time: 2540 us -> 2570 us (1.012)
    all_gather x1, waiting for transfers between devices: 70.6 us -> 163 us  [body(): lax.all_gather(values_low, 'dp', axis=0, tiled=True)]
    all_to_all x1, waiting for transfers between devices: 80.4 us -> 0.01 us  [body(): lax.all_to_all(d_rows, 'expert', split_axis=0, concat_axis=0, tiled=True)]
    unnamed x15, waiting for transfers between devices: 313 us -> 276 us
    all_to_all x0 -> x1, waiting for transfers between devices: none -> 27.2 us  [body(): lax.all_to_all(jnp.stack([values_low] * lax.axis_size('dp')), 'dp', 0, 0)]
  transfers between devices with their start and end apart: 14 -> 15, of which waited for: 14 -> 14; matrix products, arithmetic and copies ran while one was open for 8% -> 8% of each run, Pallas kernels for 0% -> 0%
where the time goes in v1:
time: 2570 us; the launch traced here: 2560 us
  waiting for transfers between devices  1750 us (68%)
  blocking collectives  237 us (9%)
  local copies, waits for them, and re-layouts  226 us (9%)
  matrix products  221 us (9%)
  other arithmetic  93.4 us (4%)
    unnamed x15, waiting for transfers between devices  276 us
    reduce_scatter x1, waiting for transfers between devices, body(): lax.psum_scatter(grad_up_part.astype(jnp.bfloat16), 'dp', scatter_dimensi...  250 us
    reduce_scatter x1, waiting for transfers between devices, body(): lax.psum_scatter(grad_gate_part.astype(jnp.bfloat16), 'dp', scatter_dimen...  250 us
    reduce_scatter x1, waiting for transfers between devices, body(): lax.psum_scatter(grad_down_part.astype(jnp.bfloat16), 'dp', scatter_dimen...  191 us
    all_gather x1, waiting for transfers between devices, body(): lax.all_gather(values_low, 'dp', axis=0, tiled=True)  163 us
    reduce_scatter x1, waiting for transfers between devices, body(): lax.psum_scatter(grad_query_part, ('dp', 'expert'), scatter_dimension=0,...  142 us
    reduce_scatter x1, waiting for transfers between devices, body(): lax.psum_scatter(grad_output_part, ('dp', 'expert'), scatter_dimension=0,...  141 us
    reduce_scatter x1, waiting for transfers between devices, body(): lax.psum_scatter(grad_value_part, ('dp', 'expert'), scatter_dimension=0,...  106 us
  transfers between devices with their start and end apart: 15, of which 14 were waited for; matrix products, arithmetic and copies ran while one was open for 8% of the time, Pallas kernels for 0%

profile of v1, /device:TPU:0, one launch (start us, length us, event | category | flops | bytes accessed | tf_op | source)
XLA Modules:
  0.0 2559.8 jit_solution(6523308436356698055)
XLA Ops:
  15.1 7.4 all-to-all-start
  32.0 9.9 scatter_custom_fusion
  41.9 13.6 gather_fusion
  56.2 11.5 reduce-window.6
  70.7 13.6 gather_fusion.1
  85.0 10.2 scatter_custom_fusion.1
  107.7 27.2 %all-to-all-done = bf16[8,320,8,64]{1,3,2,0:T(8,128)(2,1)} async-done(((bf16[8,320,8,64]{1,3,2,0:T(8,128)(2,1)}), bf16[8,320,8,64]{1,3,2,0:T(8,128)(2,1)}, u32[]{:S(2)}, u32[]{:S(2)}) %all-to-all-start) | async-done | bytes 2621472 | tf_op jit(solution)/shard_map/all_to_all | solution.py:110
  146.2 11.2 all-gather.3.cloned.1.call-done
  164.2 9.4 while.39
  175.3 10.0 while.40
  176.0 9.3 bitcast_add_fusion.5
  193.8 9.6 gather_fusion.2
  203.3 6.9 broadcast_select_fusion.1
  210.3 95.0 %all_to_all.25 = bf16[4,10,64,1536]{3,2,1,0:T(8,128)(2,1)} all-to-all(bf16[4,10,64,1536]{3,2,1,0:T(8,128)(2,1)} %broadcast_select_fusion.1), channel_id=1, replica_groups=mesh['dp'=8,'expert'=4] {'expert'}, dimensions={0} | all-to-all | bytes 15728640 | tf_op jit(solution)/shard_map/all_to_all | solution.py:174
  305.3 14.2 fusion.62
  319.5 16.7 fusion.86
  336.2 13.7 convert_bitcast_fusion
  349.9 7.2 copy.114
  364.8 85.8 %all-to-all-done.2 = bf16[4,10,64,1536]{3,2,1,0:T(8,128)(2,1)} async-done(((bf16[4,10,64,1536]{3,2,1,0:T(8,128)(2,1)}), bf16[4,10,64,1536]{3,2,1,0:T(8,128)(2,1)}, u32[]{:S(2)}, u32[]{:S(2)}) %all-to-all-start.2) | async-done | bytes 7864352 | tf_op jit(solution)/shard_map/all_to_all | solution.py:181
  457.4 20.9 gather_fusion.3
  478.3 8.0 fusion.70
  497.7 20.6 gather_fusion.4
  518.3 7.0 broadcast_select_fusion
  525.4 95.3 %all_to_all.26 = bf16[4,10,64,1536]{3,2,1,0:T(8,128)(2,1)} all-to-all(bf16[4,10,64,1536]{3,2,1,0:T(8,128)(2,1)} %broadcast_select_fusion), channel_id=1, replica_groups=mesh['dp'=8,'expert'=4] {'expert'}, dimensions={0} | all-to-all | bytes 15728640 | tf_op jit(solution)/shard_map/all_to_all | solution.py:195
  620.6 15.8 fusion.84
  636.5 11.9 fusion.56
  648.4 15.9 fusion.69
  664.2 7.3 copy.117
  678.6 163.4 %all-gather.5.cloned.1.call-done = bf16[2560,8,64]{2,1,0:T(8,128)(2,1)} async-done(((bf16[320,8,64]{2,1,0:T(8,128)(2,1)}), bf16[2560,8,64]{2,1,0:T(8,128)(2,1)}) %all-gather.5.cloned.1.call-update) | async-done | bytes 2621456 | tf_op jit(solution)/shard_map/all_gather | solution.py:260
  862.7 20.8 gather_fusion.5
  883.5 8.7 convert_reduce_fusion
  912.9 26.6 %while.41 = (s32[]{:T(128)}, f32[320,8,3,64]{0,3,2,1:T(8,128)}, f32[2560,8,64]{0,2,1:T(8,128)}, f32[2560,8,64]{0,2,1:T(8,128)}, s32[]{:T(128)}, /*index=5*/bf16[...) while((s32[]{:T(128)}, f32[320,8,3,64]{0,3,2,1:T(8,128)}, ...), condition=%wide.region_21.22_spmd.clone, body=%wide.region_20.21_spmd.clone.sunk | while | flops 2557084416 | bytes 89326328 | solution.py:297
  922.6 6.9 fusion.214
  959.9 10.7 bitcast_convert_fusion
  970.7 10.6 bitcast_convert_fusion.2
  981.4 10.6 bitcast_convert_fusion.1
  992.2 129.8 %reduce-scatter.31.cloned.1.call-done = bf16[320,512]{1,0:T(8,128)(2,1)} async-done(((bf16[2560,512]{1,0:T(8,128)(2,1)}), bf16[320,512]{1,0:T(8,128)(2,1)}) %reduce-scatter.31.cloned.1.call-update) | async-done | bytes 327696
  1127.0 67.8 %reduce-scatter.33.cloned.1.call-done = bf16[320,512]{1,0:T(8,128)(2,1)} async-done(((bf16[2560,512]{1,0:T(8,128)(2,1)}), bf16[320,512]{1,0:T(8,128)(2,1)}) %reduce-scatter.33.cloned.1.call-update) | async-done | bytes 327696
  1198.8 8.1 fusion.113
  1215.7 78.4 %reduce-scatter.35.cloned.1.call-done = f32[48,40]{1,0:T(8,128)} async-done(((f32[1536,40]{1,0:T(8,128)}), f32[48,40]{1,0:T(8,128)}) %reduce-scatter.35.cloned.1.call-update) | async-done | bytes 7696
  1304.3 46.3 %all-reduce.4 = (f32[1536]{0:T(1024)}, f32[1536]{0:T(1024)}) all-reduce(f32[1536]{0:T(1024)} %get-tuple-element.342, f32[1536]{0:T(1024)} %get-tuple-element.340), channel_id=4, replica_groups=mesh['dp'=8,'expert'=4] {'dp','expert'}, use_global_device_ids=true, to_apply=%region_26.27.clone | all-reduce | flops 3072 | bytes 24576
  1357.8 191.1 %reduce-scatter.29.cloned.1.call-done = bf16[10,64,1536]{2,1,0:T(8,128)(2,1)} async-done(((bf16[10,512,1536]{2,1,0:T(8,128)(2,1)}), bf16[10,64,1536]{2,1,0:T(8,128)(2,1)}) %reduce-scatter.29.cloned.1.call-update) | async-done | bytes 1966096 | tf_op jit(solution)/shard_map/reduce_scatter | solution.py:218
  1552.8 249.9 %reduce-scatter.25.cloned.1.call-done = bf16[10,192,512]{2,1,0:T(8,128)(2,1)} async-done(((bf16[10,1536,512]{2,1,0:T(8,128)(2,1)}), bf16[10,192,512]{2,1,0:T(8,128)(2,1)}) %reduce-scatter.25.cloned.1.call-update) | async-done | bytes 1966096 | tf_op jit(solution)/shard_map/reduce_scatter | solution.py:212
  1806.7 249.9 %reduce-scatter.27.cloned.1.call-done = bf16[10,192,512]{2,1,0:T(8,128)(2,1)} async-done(((bf16[10,1536,512]{2,1,0:T(8,128)(2,1)}), bf16[10,192,512]{2,1,0:T(8,128)(2,1)}) %reduce-scatter.27.cloned.1.call-update) | async-done | bytes 1966096 | tf_op jit(solution)/shard_map/reduce_scatter | solution.py:215
  2060.6 102.6 %reduce-scatter.19.cloned.1.call-done = f32[48,512]{1,0:T(8,128)} async-done(((f32[1536,512]{1,0:T(8,128)}), f32[48,512]{1,0:T(8,128)}) %reduce-scatter.19.cloned.1.call-update) | async-done | bytes 98320 | tf_op jit(solution)/shard_map/reduce_scatter | solution.py:347
  2163.2 106.4 %reduce-scatter.21.cloned.1.call-done = f32[48,512]{1,0:T(8,128)} async-done(((f32[1536,512]{1,0:T(8,128)}), f32[48,512]{1,0:T(8,128)}) %reduce-scatter.21.cloned.1.call-update) | async-done | bytes 98320 | tf_op jit(solution)/shard_map/reduce_scatter | solution.py:348
  2269.6 141.1 %reduce-scatter.23.cloned.1.call-done = f32[48,1536]{1,0:T(8,128)} async-done(((f32[1536,1536]{1,0:T(8,128)}), f32[48,1536]{1,0:T(8,128)}) %reduce-scatter.23.cloned.1.call-update) | async-done | bytes 294928 | tf_op jit(solution)/shard_map/reduce_scatter | solution.py:349
  2410.7 142.0 %reduce-scatter.17.cloned.1.call-done = f32[48,1536]{1,0:T(8,128)} async-done(((f32[1536,1536]{1,0:T(8,128)}), f32[48,1536]{1,0:T(8,128)}) %reduce-scatter.17.cloned.1.call-update) | async-done | bytes 294928 | tf_op jit(solution)/shard_map/reduce_scatter | solution.py:346
  (284 shorter events, 232.5 us)
Async XLA Ops:
  9.7 12.9 copy-start.50
  15.1 7.5 copy-start.5
  15.1 7.5 copy-start.41
  15.1 119.8 %all-to-all-start = ((bf16[8,320,8,64]{1,3,2,0:T(8,128)(2,1)}), bf16[8,320,8,64]{1,3,2,0:T(8,128)(2,1)}, u32[]{:S(2)}, u32[]{:S(2)}) async-start(bf16[8,320,8,64]{1,3,2,0:T(8,128)(2,1)} %stack.3), calls=%async_computation | async-start | bytes 6291456 | tf_op jit(solution)/shard_map/all_to_all | solution.py:110
  22.5 134.9 %all-gather.3.cloned.1.call-start = ((), (), s32[]{:S(2)}) async-start(), calls=%async_computation.15 | async-start | bytes 5898240 | tf_op jit(solution)/shard_map/all_gather | solution.py:108
  31.9 23.6 copy-start.54
  56.2 13.6 copy-start.55
  70.7 13.6 copy-start.58
  95.4 108.0 %copy-start.46 = (pred[4,10,64]{2,1,0:T(8,128)(4,1)}, pred[4,10,64]{2,1,0:T(8,128)(4,1)S(1)}, u32[]{:S(2)}) copy-start(pred[4,10,64]{2,1,0:T(8,128)(4,1)S(1)} %broadcast_in_dim.67) | copy-start | bytes 7684
  185.3 6.9 copy-start.3
  185.3 6.9 copy-start.56
  192.9 10.5 copy-start.59
  193.7 169.9 %copy-start.1 = (bf16[320,1536]{1,0:T(8,128)(2,1)}, bf16[320,1536]{1,0:T(8,128)(2,1)S(1)}, u32[]{:S(2)}) copy-start(bf16[320,1536]{1,0:T(8,128)(2,1)S(1)} %multiply_convert_fusion.1) | copy-start | bytes 2949124
  357.1 6.6 copy-start.33
  357.1 7.0 copy-start.38
  357.1 93.5 %all-to-all-start.2 = ((bf16[4,10,64,1536]{3,2,1,0:T(8,128)(2,1)}), bf16[4,10,64,1536]{3,2,1,0:T(8,128)(2,1)}, u32[]{:S(2)}, u32[]{:S(2)}) async-start(bf16[4,10,64,1536]{3,2,1,0:T(8,128)(2,1)} %copy.114), calls=%async_computation.2 | async-start | bytes 15728640 | tf_op jit(solution)/shard_map/all_to_all | solution.py:181
  457.4 20.9 copy-start.15
  497.7 20.6 copy-start.47
  671.5 184.3 %all-to-all-start.4 = ((bf16[4,10,64,1536]{3,2,1,0:T(8,128)(2,1)}), bf16[4,10,64,1536]{3,2,1,0:T(8,128)(2,1)}, u32[]{:S(2)}, u32[]{:S(2)}) async-start(bf16[4,10,64,1536]{3,2,1,0:T(8,128)(2,1)} %copy.117), calls=%async_computation.4 | async-start | bytes 15728640 | tf_op jit(solution)/shard_map/all_to_all | solution.py:226
  677.2 164.8 %all-gather.5.cloned.1.call-start = ((), (), s32[]{:S(2)}) async-start(), calls=%async_computation.16 | async-start | bytes 5898240 | tf_op jit(solution)/shard_map/all_gather | solution.py:260
  678.5 443.5 %reduce-scatter.31.cloned.1.call-start = ((), (), s32[]{:S(2)}) async-start(), calls=%async_computation.24 | async-start | bytes 2949120
  678.5 170.3 %copy-start.40 = (f32[320,8]{0,1:T(8,128)S(1)}, f32[320,8]{0,1:T(8,128)}, u32[]{:S(2)}) copy-start(f32[320,8]{0,1:T(8,128)} %get-tuple-element.403) | copy-start | bytes 30724
  678.5 171.1 %copy-start.44 = (f32[320,1,8]{0,2,1:T(8,128)S(1)}, f32[320,1,8]{0,2,1:T(8,128)}, u32[]{:S(2)}) copy-start(f32[320,1,8]{0,2,1:T(8,128)} %copy.138) | copy-start | bytes 30724
  678.6 171.1 %copy-start.63 = (f32[320]{0:T(512)S(1)}, f32[320]{0:T(512)}, u32[]{:S(2)}) copy-start(f32[320]{0:T(512)} %get-tuple-element.402) | copy-start | bytes 3844
  678.6 171.1 %copy-start.39 = (s32[1,320,8]{1,2,0:T(8,128)S(1)}, s32[1,320,8]{1,2,0:T(8,128)}, u32[]{:S(2)}) copy-start(s32[1,320,8]{1,2,0:T(8,128)} %param.31) | copy-start | bytes 30724
  855.9 6.8 copy-start.43
  883.5 8.7 copy-start.9
  883.5 8.7 copy-start.34
  883.5 8.7 copy-start.35
  883.5 8.7 copy-start.49
  883.5 8.7 copy-start.60
  892.3 6.1 slice-start
  948.5 246.2 %reduce-scatter.33.cloned.1.call-start = ((), (), s32[]{:S(2)}) async-start(), calls=%async_computation.25 | async-start | bytes 2949120
  957.3 336.9 %reduce-scatter.35.cloned.1.call-start = ((), (), s32[]{:S(2)}) async-start(), calls=%async_computation.26 | async-start | bytes 811008
  959.9 589.0 %reduce-scatter.29.cloned.1.call-start = ((), (), s32[]{:S(2)}) async-start(), calls=%async_computation.23 | async-start | bytes 17694720 | tf_op jit(solution)/shard_map/reduce_scatter | solution.py:218
  970.7 832.0 %reduce-scatter.25.cloned.1.call-start = ((), (), s32[]{:S(2)}) async-start(), calls=%async_computation.21 | async-start | bytes 17694720 | tf_op jit(solution)/shard_map/reduce_scatter | solution.py:212
  981.4 1075.2 %reduce-scatter.27.cloned.1.call-start = ((), (), s32[]{:S(2)}) async-start(), calls=%async_computation.22 | async-start | bytes 17694720 | tf_op jit(solution)/shard_map/reduce_scatter | solution.py:215
  992.1 131.1 %copy-start.27 = (f32[320,32]{0,1:T(8,128)S(1)}, f32[320,32]{0,1:T(8,128)}, u32[]{:S(2)}) copy-start(f32[320,32]{0,1:T(8,128)} %copy-done.25) | copy-start | bytes 122884
  992.1 131.1 %copy-start.31 = (f32[320,32]{0,1:T(8,128)S(1)}, f32[320,32]{0,1:T(8,128)}, u32[]{:S(2)}) copy-start(f32[320,32]{0,1:T(8,128)} %copy-done.29) | copy-start | bytes 122884
  992.1 132.0 %copy-start.13 = (bf16[1,320,1536]{2,1,0:T(8,128)(2,1)S(1)}, bf16[1,320,1536]{2,1,0:T(8,128)(2,1)}, u32[]{:S(2)}) copy-start(bf16[1,320,1536]{2,1,0:T(8,128)(2,1)} %multiply_convert_fusion.2) | copy-start | bytes 2949124
  992.1 1171.1 %reduce-scatter.19.cloned.1.call-start = ((), (), s32[]{:S(2)}) async-start(), calls=%async_computation.18 | async-start | bytes 3244032 | tf_op jit(solution)/shard_map/reduce_scatter | solution.py:347
  1126.9 67.8 %copy-start.7 = (f32[1,320,1536]{2,1,0:T(8,128)S(1)}, f32[1,320,1536]{2,1,0:T(8,128)}, u32[]{:S(2)}) copy-start(f32[1,320,1536]{2,1,0:T(8,128)} %param.20) | copy-start | bytes 5898244
  1126.9 67.8 %copy-start.42 = (f32[1536]{0:T(1024)S(1)}, f32[1536]{0:T(1024)}, u32[]{:S(2)}) copy-start(f32[1536]{0:T(1024)} %param.21) | copy-start | bytes 18436
  1126.9 67.8 %copy-start.51 = (f32[320]{0:T(512)S(1)}, f32[320]{0:T(512)}, u32[]{:S(2)}) copy-start(f32[320]{0:T(512)} %copy-done.50) | copy-start | bytes 3844
  1126.9 1142.7 %reduce-scatter.21.cloned.1.call-start = ((), (), s32[]{:S(2)}) async-start(), calls=%async_computation.19 | async-start | bytes 3244032 | tf_op jit(solution)/shard_map/reduce_scatter | solution.py:348
  1198.6 1212.2 %reduce-scatter.23.cloned.1.call-start = ((), (), s32[]{:S(2)}) async-start(), calls=%async_computation.20 | async-start | bytes 9732096 | tf_op jit(solution)/shard_map/reduce_scatter | solution.py:349
  1206.9 1345.8 %reduce-scatter.17.cloned.1.call-start = ((), (), s32[]{:S(2)}) async-start(), calls=%async_computation.17 | async-start | bytes 9732096 | tf_op jit(solution)/shard_map/reduce_scatter | solution.py:346
  1301.6 52.3 %copy-start.62 = (f32[320]{0:T(512)S(1)}, f32[320]{0:T(512)}, u32[]{:S(2)}) copy-start(f32[320]{0:T(512)} %get-tuple-element.422) | copy-start | bytes 3844
  (34 other events, 97.3 us)
Sparse Core Ops, SparseCore 0:
  30.9 126.4 all-gather.2
  680.8 161.1 all-gather.4
  948.6 173.3 reduce-scatter.30
  1125.3 69.3 reduce-scatter.32
  1199.7 94.4 reduce-scatter.34
  1297.6 251.2 reduce-scatter.28
  1552.4 250.2 reduce-scatter.24
  1806.3 250.2 reduce-scatter.26
  2062.6 100.5 reduce-scatter.18
  2169.1 100.4 reduce-scatter.20
  2276.1 134.5 reduce-scatter.22
  2418.1 134.6 reduce-scatter.16
